TPU v7x, 32 devices: a whole 2x2x4 slice. The times are simulated.
32 devices in a mesh: grp: 2 (over z_hi), seq: 8 (over y, x, core), tp: 2 (over z_lo).
Axes of the slice: x: 2, y: 2, z: 4 (z_hi: 2, z_lo: 2; z = z_hi * 2 + z_lo), core: 2. Of those that a mesh axis runs over, the one named last changes fastest.
Arguments:
- latents: bfloat16 [2, 64, 2048], P('grp', None, 'seq'), may hold values from -6 to 6
- patch_weight: bfloat16 [128, 5120], replicated, may hold values from -0.5 to 0.5
- patch_bias: float32 [5120], replicated, may hold values from -3 to 3
- modulation: float32 [3, 5120], replicated, may hold values from -3 to 3
- qkv_weight: bfloat16 [5120, 3, 1024], P(None, None, 'seq'), may hold values from -0.078125 to 0.078125
- norm_gain: float32 [2, 1024], P(None, 'seq'), may hold values from 0.5 to 16
- out_weight: bfloat16 [1024, 5120], P('seq', ('grp', 'tp')), may hold values from -0.5 to 0.5
- token_order: int32 [2048], replicated, may hold values from 0 to 2047, each once
- window_start: int32 [1], replicated, may hold values from 0 to 1024
Outputs:
- attended: bfloat16 [1024, 5120], P('seq', ('grp', 'tp'))
Inputs may be any that keep to these rules, and one draw needn't show every extreme that they name: Position j of the target layout holds frame-major token token_order[j]; every token stands once. The window covers target positions window_start[0] to window_start[0] + 1023.
All inputs are finite; a program needn't handle non-finite values.
Results may differ from a plain program's by a relative error of at most 0.018.
The roundings to bfloat16 on the way count: a program that leaves them out, or rounds other values in their place, can miss the bound.
Values may be sent and summed in bfloat16 or wider, within the bound.
A program may use at most 128 MiB of HBM per device.

v0:
```python
import math
import jax
import jax.numpy as jnp
from jax import lax
from jax.sharding import PartitionSpec as P

QW_DEV = 128
norm_eps = 0.1


def swapped(block, axis, apart):
    count = lax.axis_size(axis)
    route = []
    for low in range(count):
        high = low | 1 << apart
        if high != low and high < count:
            route += [(low, high), (high, low)]
    return lax.ppermute(block, axis, route)


def joined(array, axis, combine):
    everything = jax.tree.map(lambda part: lax.all_gather(part, axis), array)
    initial = jax.tree.map(lambda part: part[0], everything)

    def step(k, so_far):
        return combine(so_far, jax.tree.map(lambda part: part[k], everything))

    return lax.fori_loop(1, lax.axis_size(axis), step, initial)


def embed_rows(columns, patch_weight, patch_bias, modulation):
    channels = columns.shape[1]
    weight = patch_weight.reshape(2, channels, patch_weight.shape[1])
    embedded = (
        lax.dot_general(
            columns, weight, (((0, 1), (0, 1)), ((), ())), preferred_element_type=jnp.float32
        )
        + patch_bias
    )
    centre = embedded - jnp.mean(embedded, axis=1, keepdims=True)
    spread = jnp.mean(centre * centre, axis=1, keepdims=True)
    normed = centre * lax.rsqrt(spread + norm_eps) * (1.0 + modulation[1]) + modulation[0]
    return normed.astype(jnp.bfloat16)


def project_rows(columns, flat_weight, patch_weight, patch_bias, modulation):
    row_total = columns.shape[2]
    block = math.gcd(row_total, 512)

    def one_block(block_index):
        section = lax.dynamic_slice_in_dim(columns, block_index * block, block, 2)
        normed = embed_rows(section, patch_weight, patch_bias, modulation)
        return jnp.dot(normed, flat_weight, preferred_element_type=jnp.float32)

    result = lax.map(one_block, jnp.arange(row_total // block))
    return result.reshape(row_total, flat_weight.shape[1])


def per_device(
    latents,
    patch_weight,
    patch_bias,
    modulation,
    qkv_weight,
    norm_gain,
    out_weight,
    token_order,
    window_start,
):
    head_dim = qkv_weight.shape[2]
    seq_count = lax.axis_size("seq")
    groups = lax.axis_size("grp") * lax.axis_size("tp")
    quarter = lax.axis_index("grp") * lax.axis_size("tp") + lax.axis_index("tp")
    partner = swapped(latents, "grp", 0)
    is_high = lax.axis_index("grp") == 0
    paired = jnp.where(
        is_high, jnp.concatenate([latents, partner], 0), jnp.concatenate([partner, latents], 0)
    )
    gathered = lax.all_gather(paired, "seq", axis=2, tiled=True)
    tokens = gathered.shape[2]
    key_count = tokens // groups
    flat_weight = qkv_weight.reshape(qkv_weight.shape[0], 3 * head_dim)
    key_columns = lax.dynamic_slice_in_dim(gathered, quarter * key_count, key_count, 2)
    pair_raw = project_rows(
        key_columns, flat_weight[:, head_dim:], patch_weight, patch_bias, modulation
    )
    key_raw = pair_raw[:, :head_dim]
    values = pair_raw[:, head_dim:].astype(jnp.bfloat16)
    window_len = QW_DEV * seq_count
    window_rows = lax.dynamic_slice_in_dim(token_order, window_start[0], window_len)
    part_len = window_len // groups
    query_rows = lax.dynamic_slice_in_dim(window_rows, quarter * part_len, part_len)
    query_columns = jnp.take(gathered, query_rows, axis=2)
    query_raw = project_rows(
        query_columns, flat_weight[:, :head_dim], patch_weight, patch_bias, modulation
    )
    query_total, key_total = lax.psum(
        (jnp.sum(query_raw * query_raw, axis=1), jnp.sum(key_raw * key_raw, axis=1)), "seq"
    )
    norm_width = head_dim * seq_count
    queries = (
        query_raw * lax.rsqrt(query_total[:, None] / norm_width + norm_eps) * norm_gain[0]
    ).astype(jnp.bfloat16)
    key_rows = (
        key_raw * lax.rsqrt(key_total[:, None] / norm_width + norm_eps) * norm_gain[1]
    ).astype(jnp.bfloat16)
    queries = lax.all_gather(queries, ("grp", "tp"), axis=0, tiled=True)
    query_len = queries.shape[0]
    query_block = math.gcd(query_len, 512)
    score_scale = head_dim ** (-0.5)

    def attend(block_index):
        query_part = lax.dynamic_slice_in_dim(queries, block_index * query_block, query_block, 0)
        scores = (
            lax.dot_general(
                query_part, key_rows, (((1,), (1,)), ((), ())), preferred_element_type=jnp.float32
            )
            * score_scale
        )
        row_max = jnp.max(scores, axis=1)
        probs = jnp.exp(scores - row_max[:, None])
        row_sum = jnp.sum(probs, axis=1)
        row_acc = jnp.dot(probs.astype(jnp.bfloat16), values, preferred_element_type=jnp.float32)
        return (row_max, row_sum, row_acc)

    maxima, sums, accums = lax.map(attend, jnp.arange(query_len // query_block))
    maxima = maxima.reshape(query_len)
    sums = sums.reshape(query_len)
    accums = accums.reshape(query_len, head_dim)

    def combine(first, second):
        row_max = jnp.maximum(first[0], second[0])
        first_factor = jnp.exp(first[0] - row_max)
        second_factor = jnp.exp(second[0] - row_max)
        row_sum = first[1] * first_factor + second[1] * second_factor
        row_acc = first[2] * first_factor[:, None] + second[2] * second_factor[:, None]
        return (row_max, row_sum, row_acc)

    row_max, row_sum, row_acc = joined((maxima, sums, accums), ("grp", "tp"), combine)
    attention = (row_acc / row_sum[:, None]).astype(jnp.bfloat16)
    cols_dev = out_weight.shape[1]
    gate_cols = lax.dynamic_slice_in_dim(modulation[2], quarter * cols_dev, cols_dev)
    regrouped = lax.all_to_all(attention, "seq", split_axis=0, concat_axis=1, tiled=True)
    mixed_out = jnp.dot(
        regrouped,
        lax.all_gather(out_weight, "seq", axis=0, tiled=True),
        preferred_element_type=jnp.float32,
    )
    return (mixed_out * gate_cols).astype(jnp.bfloat16)


def solution(mesh):
    in_specs = (
        P("grp", None, "seq"),
        P(),
        P(),
        P(),
        P(None, None, "seq"),
        P(None, "seq"),
        P("seq", ("grp", "tp")),
        P(),
        P(),
    )
    out_specs = P("seq", ("grp", "tp"))
    return jax.shard_map(
        per_device, mesh=mesh, in_specs=in_specs, out_specs=out_specs, check_vma=False
    )
```

profile of v0, /device:TPU:0, one launch (start us, length us, event | category | flops | bytes accessed | tf_op | source)
XLA Modules:
  0.0 168.9 jit_solution(8679716140680726561)
XLA Ops:
  6.5 0.0 copy-start
  6.5 0.0 all-gather.5.cloned.1.call-start
  6.5 4.1 %collective-permute-start = (bf16[1,64,256]{2,1,0:T(8,128)(2,1)}, bf16[1,64,256]{2,1,0:T(8,128)(2,1)S(1)}, u32[]{:S(2)}, u32[]{:S(2)}) collective-permute-start(bf16[1,64,256]{2,1,0:T(8,128)(2,1)} %param.13), channel_id=1, source_target_pairs={{0,16},{16,0},{1,17},{17,1},{2,18},{18,2},{3,19},{19,3},{4,20},{20... | collective-permute-start | bytes 98312 | tf_op jit(solution)/shard_map/ppermute | solution.py:18
  11.3 1.7 %fusion.22 = (f32[1,5120]{1,0:T(1,128)}, f32[1,5120]{1,0:T(1,128)S(1)}, f32[1,5120]{1,0:T(1,128)S(1)}) fusion(f32[3,5120]{1,0:T(4,128)} %param.16), kind=kLoop, calls=%fused_computation.62 | loop fusion | flops 5120 | bytes 122880 | tf_op jit(solution)/shard_map/slice | solution.py:142
  13.0 1.3 slice_bitcast_fusion.1
  14.4 1.3 compare_and_fusion
  15.7 6.3 %copy.28 = bf16[5120,3,128]{0,2,1:T(8,128)(2,1)} copy(bf16[5120,3,128]{2,0,1:T(8,128)(2,1)} %param.17) | data formatting | bytes 7864320 | tf_op args[4]
  22.0 0.0 collective-permute-done
  22.0 0.0 copy-done.4
  22.0 10.9 %all_gather.18 = bf16[2,64,2048]{2,1,0:T(8,128)(2,1)S(1)} all-gather(bf16[2,64,256]{2,1,0:T(8,128)(2,1)S(1)} %maximum_select_fusion), channel_id=1, replica_groups=mesh['grp'=2,'seq'=8,'tp'=2] {'seq'}, dimensions={2}, use_global_device_ids=true | all-gather | bytes 589824 | tf_op jit(solution)/shard_map/all_gather | solution.py:79
  33.0 0.7 copy.26
  33.7 0.0 copy-done
  33.7 0.0 copy-done.3
  33.7 1.6 fusion.9
  35.4 1.6 multiply_reduce_fusion
  37.0 0.0 copy-done.5
  37.0 0.0 copy-done.7
  37.0 0.5 copy-done.1
  37.5 2.5 %fusion.11 = f32[512,256]{0,1:T(8,128)S(1)} fusion(f32[512,5120,1]{1,0,2:T(8,128)S(1)} %get-tuple-element.357, f32[5120]{0:T(1024)S(1)} %bitcast.97, f32[5120]{0:T(1024)S(1)} %bitcast.95, f32[512]{0:T(512)S(1)} %add_rsqrt_fusion.1, f32[512]{0:T(512)S(1)} %broadcast_multiply_fusion, f32[5120]{0:T(1024)S(1)} %copy-done.3, bf16[5120,384]{0,1:T(8,128)(2,1)S(1)} %bitcast.83), kind=kOutput, calls=%fused_computation.26 | convolution fusion | flops 1357905920 | bytes 13697024 | tf_op jit(solution)/shard_map/while/body/eval_jaxpr/dot_general | solution.py:53
  40.1 1.6 gather_fusion
  41.7 1.2 fusion.19
  42.9 0.0 copy-start.6
  42.9 0.0 copy-start.8
  42.9 1.7 %fusion.23 = (f32[256]{0:T(256)S(1)}, f32[256,5120]{1,0:T(8,128)S(1)}) fusion(f32[5120]{0:T(1024)} %param.15, bf16[2,64,5120]{2,1,0:T(8,128)(2,1)S(1)} %bitcast.80, bf16[2,64,256]{1,0,2:T(2,128)(2,1)S(1)} %fusion.19), kind=kOutput, calls=%fused_computation.63 | convolution fusion | flops 338165504 | bytes 6640640 | tf_op jit(solution)/shard_map/while/body/eval_jaxpr/dot_general | solution.py:35
  44.6 0.7 multiply_reduce_fusion.1
  45.3 0.0 copy-start.9
  45.3 0.0 copy-done.6
  45.4 0.0 copy-done.8
  45.4 2.6 %multiply_reduce_fusion.3 = (f32[256]{0:T(256)S(1)}, f32[256,128]{0,1:T(8,128)S(1)}) fusion(bf16[5120,384]{0,1:T(8,128)(2,1)} %bitcast.82, f32[256,5120]{1,0:T(8,128)S(1)} %get-tuple-element.353, f32[5120]{0:T(1024)S(1)} %bitcast.98, f32[5120]{0:T(1024)S(1)} %bitcast.96, f32[256]{0:T(256)S(1)} %add_rsqrt_fusion.3, f32[256]{0:T(256)S(1)} %broadcast_multiply_fusion.1), kind=kOutput, calls=%fused_computation.42 | convolution fusion | flops 342163200 | bytes 6728704 | tf_op jit(solution)/shard_map/while/body/eval_jaxpr/dot_general | solution.py:53
  47.9 13.2 %all-reduce = (f32[256]{0:T(256)S(1)}, f32[512]{0:T(512)S(1)}) all-reduce(f32[256]{0:T(256)S(1)} %get-tuple-element.354, f32[512]{0:T(512)S(1)} %multiply_reduce_fusion.2), channel_id=1, replica_groups=mesh['grp'=2,'seq'=8,'tp'=2] {'seq'}, use_global_device_ids=true, to_apply=%region_3.4 | all-reduce | flops 768 | bytes 6144 | tf_op jit(solution)/shard_map/psum | solution.py:97
  61.1 0.1 multiply_convert_fusion
  61.2 0.1 copy.30
  61.4 0.1 multiply_convert_fusion.1
  61.5 14.4 %all_gather.19 = bf16[1024,128]{0,1:T(8,128)(2,1)S(1)} all-gather(bf16[256,128]{0,1:T(8,128)(2,1)S(1)} %multiply_convert_fusion.1), channel_id=1, replica_groups=mesh['grp'=2,'seq'=8,'tp'=2] {'grp','tp'}, dimensions={0}, use_global_device_ids=true | all-gather | bytes 327680 | tf_op jit(solution)/shard_map/all_gather | solution.py:107
  75.9 0.1 copy.31
  76.0 4.4 %while.11 = (s32[]{:T(128)}, f32[2,512]{1,0:T(2,128)S(1)}, f32[2,512]{1,0:T(2,128)S(1)}, f32[2,512,128]{2,1,0:T(8,128)S(1)}, s32[2]{0:T(128)S(1)}, /*index=5*/bf...) while((s32[]{:T(128)}, f32[2,512]{1,0:T(2,128)S(1)}, ...), condition=%wide.region_11.12_spmd, body=%wide.region_8.11_spmd.sunk | while | flops 135789568 | bytes 3817663 | solution.py:126
  76.0 0.6 dynamic_slice.81
  77.2 0.3 fusion.40
  77.5 0.4 fusion.42
  77.9 0.2 fusion.41
  78.2 0.6 dynamic_slice.81
  79.5 0.3 fusion.40
  79.8 0.4 fusion.42
  80.1 0.2 fusion.41
  80.4 0.0 copy-start.2
  80.4 0.8 copy-done.2
  81.2 0.0 all-gather.5.cloned.1.call-update
  81.3 0.0 all-gather.7.cloned.1.call-start
  81.3 0.7 all-gather.7.cloned.1.call-update
  82.0 13.5 %all-gather = f32[4,1,1024]{2,1,0:T(1,128)S(1)} all-gather(f32[1,1,1024]{2,1,0:T(1,128)S(1)} %reshape.73), channel_id=1, replica_groups=mesh['grp'=2,'seq'=8,'tp'=2] {'grp','tp'}, dimensions={0}, use_global_device_ids=true | all-gather | bytes 20480 | tf_op jit(solution)/shard_map/all_gather | solution.py:22
  95.6 13.8 %all-gather.1 = f32[4,1,1024]{2,1,0:T(1,128)S(1)} all-gather(f32[1,1,1024]{2,1,0:T(1,128)S(1)} %reshape.75), channel_id=1, replica_groups=mesh['grp'=2,'seq'=8,'tp'=2] {'grp','tp'}, dimensions={0}, use_global_device_ids=true | all-gather | bytes 20480 | tf_op jit(solution)/shard_map/all_gather | solution.py:22
  109.4 16.2 %all-gather.5.cloned.1.call-done = f32[4,1024,128]{2,1,0:T(8,128)} async-done(((f32[1,1024,128]{2,1,0:T(8,128)}), f32[4,1024,128]{2,1,0:T(8,128)}) %all-gather.5.cloned.1.call-update) | async-done | bytes 2097168 | tf_op jit(solution)/shard_map/all_gather | solution.py:22
  125.6 1.1 slice_bitcast_fusion
  126.7 4.7 %while.42 = (s32[]{:T(128)}, f32[1024]{0:T(1024)S(1)}, f32[1024]{0:T(1024)S(1)}, f32[1024,128]{1,0:T(8,128)S(1)}, f32[4,1024]{1,0:T(4,128)S(1)}, /*index=5*/f32[...) while((s32[]{:T(128)}, f32[1024]{0:T(1024)S(1)}, f32[1024]{0:T(1024)S(1)}, ...), condition=%wide.region_13.14_spmd, body=%wide.region_12.13_spmd.sunk | while | flops 399365 | bytes 1630359 | solution.py:28
  126.8 1.5 fusion.43
  128.3 1.5 fusion.43
  129.9 1.5 fusion.43
  131.4 0.9 divide_convert_fusion
  132.3 3.6 %all-to-all-start = ((bf16[8,128,128]{2,1,0:T(8,128)(2,1)}), bf16[8,128,128]{2,1,0:T(8,128)(2,1)S(1)}, u32[]{:S(2)}, u32[]{:S(2)}) async-start(bf16[8,128,128]{2,1,0:T(8,128)(2,1)} %bitcast.21), calls=%async_computation | async-start | bytes 524288 | tf_op jit(solution)/shard_map/all_to_all | solution.py:143
  135.9 0.7 dynamic-slice_reduce_fusion
  136.6 7.0 %all-to-all-done = bf16[8,128,128]{2,1,0:T(8,128)(2,1)S(1)} async-done(((bf16[8,128,128]{2,1,0:T(8,128)(2,1)}), bf16[8,128,128]{2,1,0:T(8,128)(2,1)S(1)}, u32[]{:S(2)}, u32[]{:S(2)}) %all-to-all-start) | async-done | bytes 262176 | tf_op jit(solution)/shard_map/all_to_all | solution.py:143
  143.6 0.2 copy.32
  143.8 15.3 %all-gather.7.cloned.1.call-done = bf16[1024,1280]{1,0:T(8,128)(2,1)} async-done(((bf16[128,1280]{1,0:T(8,128)(2,1)}), bf16[1024,1280]{1,0:T(8,128)(2,1)}) %all-gather.7.cloned.1.call-update) | async-done | bytes 2621456 | tf_op jit(solution)/shard_map/all_gather | solution.py:146
  159.1 3.0 %fusion.14 = bf16[128,1280]{1,0:T(8,128)(2,1)} fusion(bf16[128,1024]{0,1:T(8,128)(2,1)S(1)} %bitcast.84, bf16[1024,1280]{1,0:T(8,128)(2,1)} %all-gather.7.cloned.1.call-done, f32[1280]{0:T(1024)S(1)} %dynamic-slice_reduce_fusion), kind=kOutput, calls=%fused_computation.30 | convolution fusion | flops 335872000 | bytes 3216384 | tf_op jit(solution)/shard_map/dot_general | solution.py:144
  (38 shorter events, 0.4 us)
Async XLA Ops:
  6.5 27.2 %copy-start = (bf16[128,5120]{1,0:T(8,128)(2,1)S(1)}, bf16[128,5120]{1,0:T(8,128)(2,1)}, u32[]{:S(2)}) copy-start(bf16[128,5120]{1,0:T(8,128)(2,1)} %param.14) | copy-start | bytes 3932164
  6.5 15.5 %copy-start.4 = (bf16[1,64,256]{2,1,0:T(8,128)(2,1)S(1)}, bf16[1,64,256]{2,1,0:T(8,128)(2,1)}, u32[]{:S(2)}) copy-start(bf16[1,64,256]{2,1,0:T(8,128)(2,1)} %param.13) | copy-start | bytes 98308
  6.5 27.2 %copy-start.3 = (f32[5120]{0:T(1024)S(1)}, f32[5120]{0:T(1024)}, u32[]{:S(2)}) copy-start(f32[5120]{0:T(1024)} %param.15) | copy-start | bytes 61444
  6.5 119.1 %all-gather.5.cloned.1.call-start = ((), (), s32[]{:S(2)}) async-start(), calls=%async_computation.1 | async-start | bytes 2621440 | tf_op jit(solution)/shard_map/all_gather | solution.py:22
  6.5 15.5 %collective-permute-start = (bf16[1,64,256]{2,1,0:T(8,128)(2,1)}, bf16[1,64,256]{2,1,0:T(8,128)(2,1)S(1)}, u32[]{:S(2)}, u32[]{:S(2)}) collective-permute-start(bf16[1,64,256]{2,1,0:T(8,128)(2,1)} %param.13), channel_id=1, source_target_pairs={{0,16},{16,0},{1,17},{17,1},{2,18},{18,2},{3,19},{19,3},{4,20},{20... | collective-permute-start | bytes 98312 | tf_op jit(solution)/shard_map/ppermute | solution.py:18
  13.0 23.9 %copy-start.5 = (f32[1,5120]{1,0:T(1,128)}, f32[1,5120]{1,0:T(1,128)S(1)}, u32[]{:S(2)}) copy-start(f32[1,5120]{1,0:T(1,128)S(1)} %get-tuple-element.348) | copy-start | bytes 61444
  13.0 24.0 %copy-start.7 = (f32[1,5120]{1,0:T(1,128)}, f32[1,5120]{1,0:T(1,128)S(1)}, u32[]{:S(2)}) copy-start(f32[1,5120]{1,0:T(1,128)S(1)} %get-tuple-element.349) | copy-start | bytes 61444
  35.4 2.1 %copy-start.1 = (bf16[5120,3,128]{0,2,1:T(8,128)(2,1)S(1)}, bf16[5120,3,128]{0,2,1:T(8,128)(2,1)}, u32[]{:S(2)}) copy-start(bf16[5120,3,128]{0,2,1:T(8,128)(2,1)} %copy.28) | copy-start | bytes 11796484
  42.9 2.4 %copy-start.6 = (f32[1,5120]{1,0:T(1,128)S(1)}, f32[1,5120]{1,0:T(1,128)}, u32[]{:S(2)}) copy-start(f32[1,5120]{1,0:T(1,128)} %copy-done.5) | copy-start | bytes 61444
  42.9 2.4 %copy-start.8 = (f32[1,5120]{1,0:T(1,128)S(1)}, f32[1,5120]{1,0:T(1,128)}, u32[]{:S(2)}) copy-start(f32[1,5120]{1,0:T(1,128)} %copy-done.7) | copy-start | bytes 61444
  45.3 15.8 %copy-start.10 = (f32[128]{0:T(128)S(1)}, f32[128]{0:T(128)}, u32[]{:S(2)}) copy-start(f32[128]{0:T(128)} %get-tuple-element.350) | copy-start | bytes 1540
  45.3 16.0 %copy-start.9 = (f32[128]{0:T(128)S(1)}, f32[128]{0:T(128)}, u32[]{:S(2)}) copy-start(f32[128]{0:T(128)} %get-tuple-element.351) | copy-start | bytes 1540
  80.4 0.8 copy-start.2
  81.3 77.8 %all-gather.7.cloned.1.call-start = ((), (), s32[]{:S(2)}) async-start(), calls=%async_computation.2 | async-start | bytes 2949120 | tf_op jit(solution)/shard_map/all_gather | solution.py:146
  132.3 11.3 %all-to-all-start = ((bf16[8,128,128]{2,1,0:T(8,128)(2,1)}), bf16[8,128,128]{2,1,0:T(8,128)(2,1)S(1)}, u32[]{:S(2)}, u32[]{:S(2)}) async-start(bf16[8,128,128]{2,1,0:T(8,128)(2,1)} %bitcast.21), calls=%async_computation | async-start | bytes 524288 | tf_op jit(solution)/shard_map/all_to_all | solution.py:143
Sparse Core Ops, SparseCore 0:
  81.4 44.2 all-gather.4
  127.5 31.5 all-gather.6
where the time goes:
time: 170 us; the launch traced here: 169 us
  blocking collectives  65.9 us (39%)
  waiting for transfers between devices  39.2 us (23%)
  local copies, waits for them, and re-layouts  15 us (9%)
  between operations  14.3 us (8%)
  matrix products  12.8 us (8%)
  other arithmetic  12.6 us (7%)
  starting transfers between devices  7.78 us (5%)
    all_gather x2, blocking collectives, joined(): everything = jax.tree.map(lambda part: lax.all_gather(part, axis), array)  27.3 us
    all_gather x1, waiting for transfers between devices, joined(): everything = jax.tree.map(lambda part: lax.all_gather(part, axis), array)  16.2 us
    all_gather x1, waiting for transfers between devices, per_device(): lax.all_gather(out_weight, 'seq', axis=0, tiled=True)  15.3 us
    all_gather x1, blocking collectives, per_device(): queries = lax.all_gather(queries, ('grp', 'tp'), axis=0, tiled=True)  14.4 us
    psum x1, blocking collectives, per_device(): lax.psum((jnp.sum(query_raw * query_raw, axis=1), jnp.sum(key_raw * key_r...  13.2 us
    all_gather x1, blocking collectives, per_device(): gathered = lax.all_gather(paired, 'seq', axis=2, tiled=True)  10.9 us
    unnamed x27, local copies, waits for them, and re-layouts  7.73 us
    all_to_all x1, waiting for transfers between devices, per_device(): lax.all_to_all(attention, 'seq', split_axis=0, concat_axis=1, tiled=True)  6.96 us
  transfers between devices with their start and end apart: 4, of which 3 were waited for; matrix products, arithmetic and copies ran while one was open for 11% of the time, Pallas kernels for 0%

commit v1 on v0

--- a/solution.py
+++ b/solution.py
@@ -76,7 +76,10 @@
     paired = jnp.where(
         is_high, jnp.concatenate([latents, partner], 0), jnp.concatenate([partner, latents], 0)
     )
-    gathered = lax.all_gather(paired, "seq", axis=2, tiled=True)
+    size = lax.axis_size("seq")
+    tiles = jnp.stack([paired for _ in range(size)])
+    tiles = lax.all_to_all(tiles, "seq", split_axis=0, concat_axis=0)
+    gathered = jnp.concatenate(tiles, axis=2)
     tokens = gathered.shape[2]
     key_count = tokens // groups
     flat_weight = qkv_weight.reshape(qkv_weight.shape[0], 3 * head_dim)

time: 170 us -> 168 us (0.988)
  blocking collectives: 65.9 us -> 56 us
  starting transfers between devices: 7.78 us -> 11.7 us
  waiting for transfers between devices: 39.2 us -> 42.4 us
    all_gather x1 -> x0, blocking collectives: 10.9 us -> none  [per_device(): gathered = lax.all_gather(paired, 'seq', axis=2, tiled=True)]
    all_to_all x0 -> x1, starting transfers between devices: none -> 3.93 us  [per_device(): tiles = lax.all_to_all(tiles, 'seq', split_axis=0, concat_axis=0)]
    ppermute x1, waiting for transfers between devices: 0.01 us -> 2.45 us  [swapped(): return lax.ppermute(block, axis, route)]
  transfers between devices with their start and end apart: 4 -> 5, of which waited for: 3 -> 4; matrix products, arithmetic and copies ran while one was open for 11% -> 10% of each run, Pallas kernels for 0% -> 0%
where the time goes in v1:
time: 168 us; the launch traced here: 167 us
  blocking collectives  56 us (33%)
  waiting for transfers between devices  42.4 us (25%)
  local copies, waits for them, and re-layouts  15.1 us (9%)
  between operations  14.3 us (9%)
  other arithmetic  13.5 us (8%)
  matrix products  12.8 us (8%)
  starting transfers between devices  11.7 us (7%)
    all_gather x2, blocking collectives, joined(): everything = jax.tree.map(lambda part: lax.all_gather(part, axis), array)  27.3 us
    all_gather x1, waiting for transfers between devices, joined(): everything = jax.tree.map(lambda part: lax.all_gather(part, axis), array)  17 us
    all_gather x1, waiting for transfers between devices, per_device(): lax.all_gather(out_weight, 'seq', axis=0, tiled=True)  15.3 us
    psum x1, blocking collectives, per_device(): lax.psum((jnp.sum(query_raw * query_raw, axis=1), jnp.sum(key_raw * key_r...  14.4 us
    all_gather x1, blocking collectives, per_device(): queries = lax.all_gather(queries, ('grp', 'tp'), axis=0, tiled=True)  14.3 us
    unnamed x27, local copies, waits for them, and re-layouts  7.69 us
    all_to_all x1, waiting for transfers between devices, per_device(): lax.all_to_all(attention, 'seq', split_axis=0, concat_axis=1, tiled=True)  6.94 us
    dot_general x2, matrix products, one_block(): return jnp.dot(normed, flat_weight, preferred_element_type=jnp.float32)  5.05 us
  transfers between devices with their start and end apart: 5, of which 4 were waited for; matrix products, arithmetic and copies ran while one was open for 10% of the time, Pallas kernels for 0%

profile of v1, /device:TPU:0, one launch (start us, length us, event | category | flops | bytes accessed | tf_op | source)
XLA Modules:
  0.0 167.2 jit_solution(10222009172009704403)
XLA Ops:
  6.5 0.0 copy-start
  6.5 4.1 %collective-permute-start = (bf16[1,64,256]{2,1,0:T(8,128)(2,1)}, bf16[1,64,256]{2,1,0:T(8,128)(2,1)S(1)}, u32[]{:S(2)}, u32[]{:S(2)}) collective-permute-start(bf16[1,64,256]{2,1,0:T(8,128)(2,1)} %param.13), channel_id=1, source_target_pairs={{0,16},{16,0},{1,17},{17,1},{2,18},{18,2},{3,19},{19,3},{4,20},{20... | collective-permute-start | bytes 98312 | tf_op jit(solution)/shard_map/ppermute | solution.py:18
  10.6 2.5 %collective-permute-done = bf16[1,64,256]{2,1,0:T(8,128)(2,1)S(1)} collective-permute-done((bf16[1,64,256]{2,1,0:T(8,128)(2,1)}, bf16[1,64,256]{2,1,0:T(8,128)(2,1)S(1)}, u32[]{:S(2)}, u32[]{:S(2)}) %collective-permute-start) | collective-permute-done | bytes 32800 | tf_op jit(solution)/shard_map/ppermute | solution.py:18
  13.1 0.8 maximum_select_fusion
  13.9 0.8 stack.2
  14.7 3.9 %all-to-all-start = ((bf16[8,2,64,256]{3,2,1,0:T(8,128)(2,1)}), bf16[8,2,64,256]{3,2,1,0:T(8,128)(2,1)S(1)}, u32[]{:S(2)}, u32[]{:S(2)}) async-start(bf16[8,2,64,256]{3,2,1,0:T(8,128)(2,1)} %stack.2), calls=%async_computation | async-start | bytes 1048576 | tf_op jit(solution)/shard_map/all_to_all | solution.py:81
  18.7 0.0 all-gather.5.cloned.1.call-start
  18.7 1.7 %fusion.22 = (f32[1,5120]{1,0:T(1,128)}, f32[1,5120]{1,0:T(1,128)S(1)}, f32[1,5120]{1,0:T(1,128)S(1)}) fusion(f32[3,5120]{1,0:T(4,128)} %param.16), kind=kLoop, calls=%fused_computation.62 | loop fusion | flops 5120 | bytes 122880 | tf_op jit(solution)/shard_map/slice | solution.py:145
  21.1 0.0 copy-start.3
  21.1 6.3 %copy.29 = bf16[5120,3,128]{0,2,1:T(8,128)(2,1)} copy(bf16[5120,3,128]{2,0,1:T(8,128)(2,1)} %param.17) | data formatting | bytes 7864320 | tf_op args[4]
  27.4 1.4 compare_and_fusion
  28.8 0.0 copy-done.10
  28.8 0.6 slice_bitcast_fusion.1
  29.4 0.0 all-to-all-done
  29.4 0.8 copy.27
  30.2 1.6 fusion.9
  31.9 1.6 multiply_reduce_fusion
  33.5 0.5 copy-done.1
  34.0 2.5 %fusion.11 = f32[512,256]{0,1:T(8,128)S(1)} fusion(f32[512,5120,1]{1,0,2:T(8,128)S(1)} %get-tuple-element.357, f32[5120]{0:T(1024)S(1)} %bitcast.103, f32[5120]{0:T(1024)S(1)} %bitcast.101, f32[512]{0:T(512)S(1)} %add_rsqrt_fusion.1, f32[512]{0:T(512)S(1)} %broadcast_multiply_fusion, f32[5120]{0:T(1024)S(1)} %copy-done.3, bf16[5120,384]{0,1:T(8,128)(2,1)S(1)} %bitcast.86), kind=kOutput, calls=%fused_computation.26 | convolution fusion | flops 1357905920 | bytes 13697024 | tf_op jit(solution)/shard_map/while/body/eval_jaxpr/dot_general | solution.py:53
  36.5 1.6 gather_fusion
  38.1 1.2 fusion.19
  39.4 0.0 copy-start.5
  39.4 0.0 copy-start.7
  39.4 1.7 %fusion.23 = (f32[256]{0:T(256)S(1)}, f32[256,5120]{1,0:T(8,128)S(1)}) fusion(f32[5120]{0:T(1024)} %param.15, bf16[2,64,5120]{2,1,0:T(8,128)(2,1)S(1)} %bitcast.83, bf16[2,64,256]{1,0,2:T(2,128)(2,1)S(1)} %fusion.19), kind=kOutput, calls=%fused_computation.63 | convolution fusion | flops 338165504 | bytes 6640640 | tf_op jit(solution)/shard_map/while/body/eval_jaxpr/dot_general | solution.py:35
  41.1 0.7 multiply_reduce_fusion.1
  41.8 0.0 copy-done.5
  41.8 0.0 copy-done.7
  41.8 2.6 %multiply_reduce_fusion.3 = (f32[256]{0:T(256)S(1)}, f32[256,128]{0,1:T(8,128)S(1)}) fusion(bf16[5120,384]{0,1:T(8,128)(2,1)} %bitcast.85, f32[256,5120]{1,0:T(8,128)S(1)} %get-tuple-element.353, f32[5120]{0:T(1024)S(1)} %bitcast.104, f32[5120]{0:T(1024)S(1)} %bitcast.102, f32[256]{0:T(256)S(1)} %add_rsqrt_fusion.3, f32[256]{0:T(256)S(1)} %broadcast_multiply_fusion.1), kind=kOutput, calls=%fused_computation.42 | convolution fusion | flops 342163200 | bytes 6728704 | tf_op jit(solution)/shard_map/while/body/eval_jaxpr/dot_general | solution.py:53
  44.4 14.4 %all-reduce = (f32[256]{0:T(256)S(1)}, f32[512]{0:T(512)S(1)}) all-reduce(f32[256]{0:T(256)S(1)} %get-tuple-element.354, f32[512]{0:T(512)S(1)} %multiply_reduce_fusion.2), channel_id=1, replica_groups=mesh['grp'=2,'seq'=8,'tp'=2] {'seq'}, use_global_device_ids=true, to_apply=%region_3.4 | all-reduce | flops 768 | bytes 6144 | tf_op jit(solution)/shard_map/psum | solution.py:100
  58.8 0.1 multiply_convert_fusion
  58.9 0.1 copy.31
  59.0 0.0 copy-done.8
  59.0 0.1 multiply_convert_fusion.1
  59.1 14.3 %all_gather.15 = bf16[1024,128]{0,1:T(8,128)(2,1)S(1)} all-gather(bf16[256,128]{0,1:T(8,128)(2,1)S(1)} %multiply_convert_fusion.1), channel_id=1, replica_groups=mesh['grp'=2,'seq'=8,'tp'=2] {'grp','tp'}, dimensions={0}, use_global_device_ids=true | all-gather | bytes 327680 | tf_op jit(solution)/shard_map/all_gather | solution.py:110
  73.4 0.1 copy.32
  73.6 4.4 %while.11 = (s32[]{:T(128)}, f32[2,512]{1,0:T(2,128)S(1)}, f32[2,512]{1,0:T(2,128)S(1)}, f32[2,512,128]{2,1,0:T(8,128)S(1)}, s32[2]{0:T(128)S(1)}, /*index=5*/bf...) while((s32[]{:T(128)}, f32[2,512]{1,0:T(2,128)S(1)}, ...), condition=%wide.region_11.12_spmd, body=%wide.region_8.11_spmd.sunk | while | flops 135789568 | bytes 3817663 | solution.py:129
  73.6 0.6 dynamic_slice.81
  74.8 0.3 fusion.40
  75.1 0.4 fusion.42
  75.5 0.2 fusion.41
  75.8 0.6 dynamic_slice.81
  77.0 0.3 fusion.40
  77.3 0.4 fusion.42
  77.7 0.2 fusion.41
  78.0 0.0 copy-start.2
  78.0 0.8 copy-done.2
  78.8 0.0 all-gather.5.cloned.1.call-update
  78.8 0.0 all-gather.7.cloned.1.call-start
  78.9 0.7 all-gather.7.cloned.1.call-update
  79.6 13.5 %all-gather = f32[4,1,1024]{2,1,0:T(1,128)S(1)} all-gather(f32[1,1,1024]{2,1,0:T(1,128)S(1)} %reshape.94), channel_id=1, replica_groups=mesh['grp'=2,'seq'=8,'tp'=2] {'grp','tp'}, dimensions={0}, use_global_device_ids=true | all-gather | bytes 20480 | tf_op jit(solution)/shard_map/all_gather | solution.py:22
  93.1 13.9 %all-gather.1 = f32[4,1,1024]{2,1,0:T(1,128)S(1)} all-gather(f32[1,1,1024]{2,1,0:T(1,128)S(1)} %reshape.96), channel_id=1, replica_groups=mesh['grp'=2,'seq'=8,'tp'=2] {'grp','tp'}, dimensions={0}, use_global_device_ids=true | all-gather | bytes 20480 | tf_op jit(solution)/shard_map/all_gather | solution.py:22
  107.0 17.0 %all-gather.5.cloned.1.call-done = f32[4,1024,128]{2,1,0:T(8,128)} async-done(((f32[1,1024,128]{2,1,0:T(8,128)}), f32[4,1024,128]{2,1,0:T(8,128)}) %all-gather.5.cloned.1.call-update) | async-done | bytes 2097168 | tf_op jit(solution)/shard_map/all_gather | solution.py:22
  124.0 1.1 slice_bitcast_fusion
  125.1 4.7 %while.42 = (s32[]{:T(128)}, f32[1024]{0:T(1024)S(1)}, f32[1024]{0:T(1024)S(1)}, f32[1024,128]{1,0:T(8,128)S(1)}, f32[4,1024]{1,0:T(4,128)S(1)}, /*index=5*/f32[...) while((s32[]{:T(128)}, f32[1024]{0:T(1024)S(1)}, f32[1024]{0:T(1024)S(1)}, ...), condition=%wide.region_13.14_spmd, body=%wide.region_12.13_spmd.sunk | while | flops 399365 | bytes 1630359 | solution.py:28
  125.1 1.5 fusion.43
  126.7 1.5 fusion.43
  128.2 1.5 fusion.43
  129.7 0.9 divide_convert_fusion
  130.7 3.6 %all-to-all-start.1 = ((bf16[8,128,128]{2,1,0:T(8,128)(2,1)}), bf16[8,128,128]{2,1,0:T(8,128)(2,1)S(1)}, u32[]{:S(2)}, u32[]{:S(2)}) async-start(bf16[8,128,128]{2,1,0:T(8,128)(2,1)} %bitcast.22), calls=%async_computation.1 | async-start | bytes 524288 | tf_op jit(solution)/shard_map/all_to_all | solution.py:146
  134.3 0.7 dynamic-slice_reduce_fusion
  135.0 6.9 %all-to-all-done.1 = bf16[8,128,128]{2,1,0:T(8,128)(2,1)S(1)} async-done(((bf16[8,128,128]{2,1,0:T(8,128)(2,1)}), bf16[8,128,128]{2,1,0:T(8,128)(2,1)S(1)}, u32[]{:S(2)}, u32[]{:S(2)}) %all-to-all-start.1) | async-done | bytes 262176 | tf_op jit(solution)/shard_map/all_to_all | solution.py:146
  141.9 0.2 copy.33
  142.1 15.3 %all-gather.7.cloned.1.call-done = bf16[1024,1280]{1,0:T(8,128)(2,1)} async-done(((bf16[128,1280]{1,0:T(8,128)(2,1)}), bf16[1024,1280]{1,0:T(8,128)(2,1)}) %all-gather.7.cloned.1.call-update) | async-done | bytes 2621456 | tf_op jit(solution)/shard_map/all_gather | solution.py:149
  157.4 3.0 %fusion.14 = bf16[128,1280]{1,0:T(8,128)(2,1)} fusion(bf16[128,1024]{0,1:T(8,128)(2,1)S(1)} %bitcast.90, bf16[1024,1280]{1,0:T(8,128)(2,1)} %all-gather.7.cloned.1.call-done, f32[1280]{0:T(1024)S(1)} %dynamic-slice_reduce_fusion), kind=kOutput, calls=%fused_computation.30 | convolution fusion | flops 335872000 | bytes 3216384 | tf_op jit(solution)/shard_map/dot_general | solution.py:147
  (41 shorter events, 0.4 us)
Async XLA Ops:
  6.5 23.6 %copy-start = (bf16[128,5120]{1,0:T(8,128)(2,1)S(1)}, bf16[128,5120]{1,0:T(8,128)(2,1)}, u32[]{:S(2)}) copy-start(bf16[128,5120]{1,0:T(8,128)(2,1)} %param.14) | copy-start | bytes 3932164
  6.5 22.3 %copy-start.10 = (f32[2,128]{1,0:T(2,128)S(1)}, f32[2,128]{1,0:T(2,128)}, u32[]{:S(2)}) copy-start(f32[2,128]{1,0:T(2,128)} %param.18) | copy-start | bytes 3076
  6.5 6.5 %collective-permute-start = (bf16[1,64,256]{2,1,0:T(8,128)(2,1)}, bf16[1,64,256]{2,1,0:T(8,128)(2,1)S(1)}, u32[]{:S(2)}, u32[]{:S(2)}) collective-permute-start(bf16[1,64,256]{2,1,0:T(8,128)(2,1)} %param.13), channel_id=1, source_target_pairs={{0,16},{16,0},{1,17},{17,1},{2,18},{18,2},{3,19},{19,3},{4,20},{20... | collective-permute-start | bytes 98312 | tf_op jit(solution)/shard_map/ppermute | solution.py:18
  14.7 14.6 %all-to-all-start = ((bf16[8,2,64,256]{3,2,1,0:T(8,128)(2,1)}), bf16[8,2,64,256]{3,2,1,0:T(8,128)(2,1)S(1)}, u32[]{:S(2)}, u32[]{:S(2)}) async-start(bf16[8,2,64,256]{3,2,1,0:T(8,128)(2,1)} %stack.2), calls=%async_computation | async-start | bytes 1048576 | tf_op jit(solution)/shard_map/all_to_all | solution.py:81
  18.7 105.3 %all-gather.5.cloned.1.call-start = ((), (), s32[]{:S(2)}) async-start(), calls=%async_computation.2 | async-start | bytes 2621440 | tf_op jit(solution)/shard_map/all_gather | solution.py:22
  20.4 13.0 %copy-start.4 = (f32[1,5120]{1,0:T(1,128)}, f32[1,5120]{1,0:T(1,128)S(1)}, u32[]{:S(2)}) copy-start(f32[1,5120]{1,0:T(1,128)S(1)} %get-tuple-element.348) | copy-start | bytes 61444
  20.4 13.0 %copy-start.6 = (f32[1,5120]{1,0:T(1,128)}, f32[1,5120]{1,0:T(1,128)S(1)}, u32[]{:S(2)}) copy-start(f32[1,5120]{1,0:T(1,128)S(1)} %get-tuple-element.349) | copy-start | bytes 61444
  21.1 9.1 %copy-start.3 = (f32[5120]{0:T(1024)S(1)}, f32[5120]{0:T(1024)}, u32[]{:S(2)}) copy-start(f32[5120]{0:T(1024)} %param.15) | copy-start | bytes 61444
  31.9 2.1 %copy-start.1 = (bf16[5120,3,128]{0,2,1:T(8,128)(2,1)S(1)}, bf16[5120,3,128]{0,2,1:T(8,128)(2,1)}, u32[]{:S(2)}) copy-start(bf16[5120,3,128]{0,2,1:T(8,128)(2,1)} %copy.29) | copy-start | bytes 11796484
  39.4 2.4 %copy-start.5 = (f32[1,5120]{1,0:T(1,128)S(1)}, f32[1,5120]{1,0:T(1,128)}, u32[]{:S(2)}) copy-start(f32[1,5120]{1,0:T(1,128)} %copy-done.4) | copy-start | bytes 61444
  39.4 2.4 %copy-start.7 = (f32[1,5120]{1,0:T(1,128)S(1)}, f32[1,5120]{1,0:T(1,128)}, u32[]{:S(2)}) copy-start(f32[1,5120]{1,0:T(1,128)} %copy-done.6) | copy-start | bytes 61444
  41.8 17.0 %copy-start.9 = (f32[128]{0:T(128)S(1)}, f32[128]{0:T(128)}, u32[]{:S(2)}) copy-start(f32[128]{0:T(128)} %get-tuple-element.350) | copy-start | bytes 1540
  41.8 17.2 %copy-start.8 = (f32[128]{0:T(128)S(1)}, f32[128]{0:T(128)}, u32[]{:S(2)}) copy-start(f32[128]{0:T(128)} %get-tuple-element.351) | copy-start | bytes 1540
  78.0 0.8 copy-start.2
  78.8 78.6 %all-gather.7.cloned.1.call-start = ((), (), s32[]{:S(2)}) async-start(), calls=%async_computation.3 | async-start | bytes 2949120 | tf_op jit(solution)/shard_map/all_gather | solution.py:149
  130.7 11.3 %all-to-all-start.1 = ((bf16[8,128,128]{2,1,0:T(8,128)(2,1)}), bf16[8,128,128]{2,1,0:T(8,128)(2,1)S(1)}, u32[]{:S(2)}, u32[]{:S(2)}) async-start(bf16[8,128,128]{2,1,0:T(8,128)(2,1)} %bitcast.22), calls=%async_computation.1 | async-start | bytes 524288 | tf_op jit(solution)/shard_map/all_to_all | solution.py:146
Sparse Core Ops, SparseCore 0:
  78.9 44.9 all-gather.4
  125.9 31.4 all-gather.6
